TPU v7x, 32 devices: a whole 2x2x4 slice. The times are simulated.
32 devices in a mesh: dp: 32 (over z, y, x, core).
Axes of the slice: x: 2, y: 2, z: 4, core: 2. Of those that a mesh axis runs over, the one named last changes fastest.
Arguments:
- params: float32 [1774080], P('dp')
- images: bfloat16 [256, 197, 384], P('dp'), may hold values from -6 to 6
- cotangent: bfloat16 [256, 197, 384], P('dp'), may hold values from -6 to 6
- live: int32 [32], P('dp'), may hold values from 1 to 8, as said below
Outputs:
- layer_out: bfloat16 [256, 197, 384], P('dp')
- input_grad: bfloat16 [256, 197, 384], P('dp')
- flat_parameter_gradient: float32 [1774080], P('dp')
Inputs may be any that keep to these rules, and one draw needn't show every extreme that they name: The first live[d] of device d's 8 slots hold images; every draw has a device with all 8 slots occupied.
All inputs are finite; a program needn't handle non-finite values.
Results may differ from a plain program's by a relative error of at most 0.0098.
Values may be sent and summed in bfloat16 or wider, within the bound.
A program may use at most 192 MiB of HBM per device.

v0:
```python
import functools

import jax
import jax.numpy as jnp
from jax import lax
from jax.experimental import pallas as pl
from jax.experimental.pallas import tpu as pltpu
from jax.sharding import PartitionSpec as P

D = 384
HEADS = 6
FF = 1536
HD = D // HEADS
PAIRS = HEADS // 2
EPS = 1e-06
LANES = 128
BF = jnp.bfloat16
F32 = jnp.float32

ROW_QKV = 2
ROW_OUT = 2 + 3 * D + 2
ROW_UP = ROW_OUT + D + 3
ROW_BUP = ROW_UP + FF
ROW_DOWN = ROW_BUP + FF // D
ROW_BDOWN = ROW_DOWN + FF
ROWS = ROW_BDOWN + 1
VEC_ROWS = (0, 1, ROW_OUT - 2, ROW_OUT - 1, ROW_UP - 3, ROW_UP - 2, ROW_UP - 1, ROW_BDOWN)
G1, S1, BQ, BV, BO, G2, S2, BD = range(8)

GROUP = 2
CHUNK = 512


def up_to(value, unit):
    return (value + unit - 1) // unit * unit


def nt(a, b):
    return lax.dot_general(a, b, (((1,), (1,)), ((), ())), preferred_element_type=F32)


def tn(a, b):
    return lax.dot_general(a, b, (((0,), (0,)), ((), ())), preferred_element_type=F32)


def nn(a, b):
    return jnp.dot(a, b, preferred_element_type=F32)


def norm_stats(values):
    center = values - jnp.mean(values, axis=-1, keepdims=True)
    inv = lax.rsqrt(jnp.mean(center * center, axis=-1, keepdims=True) + EPS)
    return center * inv, inv


def norm_back(grad_out, hat, inv, gain):
    g = grad_out * gain
    return inv * (
        g
        - jnp.mean(g, axis=-1, keepdims=True)
        - hat * jnp.mean(g * hat, axis=-1, keepdims=True)
    )


def colsum(v):
    return jnp.sum(v, axis=0, keepdims=True)


def matrices():
    return (
        (0, D, 9, ROW_QKV),
        (1, D, 3, ROW_OUT),
        (2, D, 12, ROW_UP),
        (3, FF, 3, ROW_DOWN),
    )


def layer_kernel(
    n, shard, tok, tokp,
    live_ref, gath_ref, img_ref, cot_ref,
    out_ref, din_ref, grad_ref,
    buf, wqkv, wout, wup, wdn, vec, bup,
    gqkv, gout, gup, gdn, gvec, gbup,
    x_s, dout_s, attn_s, qkv_s, probs_s, mixed_s, dmix_s, dqkv_s,
):
    step = pl.program_id(0)
    window = gath_ref.shape[1]
    weights = (wqkv, wout, wup, wdn)
    grads = (gqkv, gout, gup, gdn)

    @pl.when(step == 0)
    def _():
        for d in range(n):
            first, shift = divmod(shard * d, LANES)
            rows = (shift + shard + LANES - 1) // LANES
            piece = gath_ref[d].astype(F32)
            if d > 0 and shift:
                seam = buf[first : first + 1, :] + piece[0:1]
                buf[first : first + rows, :] = piece[:rows]
                buf[first : first + 1, :] = seam
            else:
                buf[first : first + rows, :] = piece[:rows]
        for k, rows, blocks, start in matrices():
            for b in range(blocks):
                weights[k][:, b * LANES : (b + 1) * LANES] = buf[
                    pl.ds(3 * start + b, rows, blocks), :
                ].astype(BF)
        for i, r in enumerate(VEC_ROWS):
            for c in range(3):
                vec[i : i + 1, c * LANES : (c + 1) * LANES] = buf[3 * r + c : 3 * r + c + 1, :]
        for c in range(FF // LANES):
            bup[:, c * LANES : (c + 1) * LANES] = buf[3 * ROW_BUP + c : 3 * ROW_BUP + c + 1, :]
        for ref in (*grads, gvec, gbup, x_s, dout_s):
            ref[...] = jnp.zeros_like(ref)

    def param(i):
        return vec[i : i + 1, :]

    def add_vec(i, value):
        gvec[i : i + 1, :] += value

    live = live_ref[0]
    masks = [(step * GROUP + g < live).astype(F32) for g in range(GROUP)]
    for g in range(GROUP):
        x_s[g * tokp : g * tokp + tok, :] = img_ref[g].astype(F32)
        dout_s[g * tokp : g * tokp + tok, :] = cot_ref[g].astype(F32) * masks[g]

    hat1, _ = norm_stats(x_s[...])
    attn_s[...] = (hat1 * param(G1) + param(S1)).astype(BF)
    attn_in = attn_s[...]
    for j, bias in enumerate((BQ, None, BV)):
        part = nn(attn_in, wqkv[:, j * D : (j + 1) * D])
        if bias is not None:
            part = part + param(bias)
        qkv_s[:, j * D : (j + 1) * D] = part.astype(BF)

    lane = lax.broadcasted_iota(jnp.int32, (1, LANES), 1)
    low = lane < HD
    low_b = low.astype(BF)
    high_b = 1 - low_b
    key_ok = lax.broadcasted_iota(jnp.int32, (1, tokp), 1) < tok

    def views(t):
        g, p = t // PAIRS, t % PAIRS
        rows = pl.ds(pl.multiple_of(g * tokp, 16), tokp)
        return rows, [pl.ds(pl.multiple_of(j * D + p * LANES, LANES), LANES) for j in range(3)]

    def stack(v):
        return jnp.concatenate([v * low_b, v * high_b], axis=0)

    def attend(t, carry):
        rows, (cq, ck, cv) = views(t)
        q, k, v = qkv_s[rows, cq], qkv_s[rows, ck], qkv_s[rows, cv]
        s = nt(stack(q), k) * (HD**-0.5)
        s = jnp.where(key_ok, s, -1e30)
        e = jnp.exp(s - jnp.max(s, axis=-1, keepdims=True))
        probs = e * (1.0 / jnp.sum(e, axis=-1, keepdims=True))
        probs_s[t] = probs
        mixed = nn(probs.astype(BF), v)
        mixed_s[rows, cq] = jnp.where(low, mixed[:tokp], mixed[tokp:]).astype(BF)
        return carry

    lax.fori_loop(0, GROUP * PAIRS, attend, 0)

    hidden = x_s[...] + nn(mixed_s[...], wout[...]) + param(BO)
    hat2, inv2 = norm_stats(hidden)
    ffn_in = (hat2 * param(G2) + param(S2)).astype(BF)
    dout = dout_s[...]
    dout_b = dout.astype(BF)
    add_vec(BD, colsum(dout))
    result = hidden + param(BD)
    dn2 = jnp.zeros_like(hidden)
    for c in range(FF // CHUNK):
        cols = slice(c * CHUNK, (c + 1) * CHUNK)
        pre = nn(ffn_in, wup[:, cols]) + bup[:, cols]
        cumul = 0.5 * (1.0 + lax.erf(pre * 0.7071067811865476))
        act = (pre * cumul).astype(BF)
        result = result + nn(act, wdn[cols, :])
        gdn[cols, :] += tn(act, dout_b)
        density = jnp.exp(-0.5 * pre * pre) * 0.3989422804014327
        dpre = nt(dout_b, wdn[cols, :]) * (cumul + pre * density)
        gbup[:, cols] += colsum(dpre)
        dpre_b = dpre.astype(BF)
        gup[:, cols] += tn(ffn_in, dpre_b)
        dn2 = dn2 + nt(dpre_b, wup[:, cols])
    for g in range(GROUP):
        out_ref[g] = (result[g * tokp : g * tokp + tok] * masks[g]).astype(BF)

    add_vec(G2, colsum(dn2 * hat2))
    add_vec(S2, colsum(dn2))
    dhidden = dout + norm_back(dn2, hat2, inv2, param(G2))
    dout_s[...] = dhidden
    dhidden_b = dhidden.astype(BF)
    add_vec(BO, colsum(dhidden))
    gout[...] += tn(mixed_s[...], dhidden_b)
    dmix_s[...] = nt(dhidden_b, wout[...]).astype(BF)

    def attend_back(t, carry):
        rows, (cq, ck, cv) = views(t)
        q, k, v = qkv_s[rows, cq], qkv_s[rows, ck], qkv_s[rows, cv]
        dm = stack(dmix_s[rows, cq])
        probs = probs_s[t]
        dprobs = nt(dm, v)
        delta = jnp.sum(probs * dprobs, axis=-1, keepdims=True)
        ds = (probs * (dprobs - delta) * (HD**-0.5)).astype(BF)
        dvalue = tn(probs.astype(BF), dm)
        dq = nn(ds, k)
        dquery = jnp.where(low, dq[:tokp], dq[tokp:])
        dkey = tn(ds, stack(q))
        gvec[BQ : BQ + 1, cq] += colsum(dquery)
        gvec[BV : BV + 1, cq] += colsum(dvalue)
        dqkv_s[rows, cq] = dquery.astype(BF)
        dqkv_s[rows, ck] = dkey.astype(BF)
        dqkv_s[rows, cv] = dvalue.astype(BF)
        return carry

    lax.fori_loop(0, GROUP * PAIRS, attend_back, 0)

    attn_in = attn_s[...]
    dn1 = jnp.zeros_like(hidden)
    for j in range(3):
        cols = slice(j * D, (j + 1) * D)
        part = dqkv_s[:, cols]
        gqkv[:, cols] += tn(attn_in, part)
        dn1 = dn1 + nt(part, wqkv[:, cols])
    hat1, inv1 = norm_stats(x_s[...])
    add_vec(G1, colsum(dn1 * hat1))
    add_vec(S1, colsum(dn1))
    dinput = dout_s[...] + norm_back(dn1, hat1, inv1, param(G1))
    for g in range(GROUP):
        din_ref[g] = dinput[g * tokp : g * tokp + tok].astype(BF)
        dout_s[g * tokp + tok : (g + 1) * tokp, :] = jnp.zeros((tokp - tok, D), F32)

    @pl.when(step == pl.num_programs(0) - 1)
    def _():
        for k, rows, blocks, start in matrices():
            for b in range(blocks):
                buf[pl.ds(3 * start + b, rows, blocks), :] = grads[k][
                    :, b * LANES : (b + 1) * LANES
                ]
        for i, r in enumerate(VEC_ROWS):
            for c in range(3):
                buf[3 * r + c : 3 * r + c + 1, :] = gvec[i : i + 1, c * LANES : (c + 1) * LANES]
        for c in range(FF // LANES):
            buf[3 * ROW_BUP + c : 3 * ROW_BUP + c + 1, :] = gbup[:, c * LANES : (c + 1) * LANES]
        tail = buf.shape[0] - 3 * ROWS
        buf[3 * ROWS :, :] = jnp.zeros((tail, LANES), F32)
        for d in range(n):
            first = shard * d // LANES
            grad_ref[d] = buf[first : first + window, :].astype(grad_ref.dtype)


def run_layer(n, shard, window, live, gathered, images, cotangent):
    slots, tok, _ = images.shape
    tokp = up_to(tok, 16)
    rows = GROUP * tokp
    buf_rows = up_to(max(shard * (n - 1) // LANES + window, 3 * ROWS) + 8, 8)
    block = pl.BlockSpec((GROUP, tok, D), lambda i: (i, 0, 0))
    whole = pl.BlockSpec(memory_space=pltpu.VMEM)
    VM = pltpu.VMEM
    return pl.pallas_call(
        functools.partial(layer_kernel, n, shard, tok, tokp),
        grid=(slots // GROUP,),
        in_specs=[pl.BlockSpec(memory_space=pltpu.SMEM), whole, block, block],
        out_specs=[block, block, whole],
        out_shape=[
            jax.ShapeDtypeStruct(images.shape, BF),
            jax.ShapeDtypeStruct(images.shape, BF),
            jax.ShapeDtypeStruct((n, window, LANES), BF),
        ],
        scratch_shapes=[
            VM((buf_rows, LANES), F32),
            VM((D, 3 * D), BF), VM((D, D), BF), VM((D, FF), BF), VM((FF, D), BF),
            VM((8, D), F32), VM((1, FF), F32),
            VM((D, 3 * D), F32), VM((D, D), F32), VM((D, FF), F32), VM((FF, D), F32),
            VM((8, D), F32), VM((1, FF), F32),
            VM((rows, D), F32), VM((rows, D), F32), VM((rows, D), BF),
            VM((rows, 3 * D), BF), VM((GROUP * PAIRS, 2 * tokp, tokp), F32),
            VM((rows, D), BF), VM((rows, D), BF), VM((rows, 3 * D), BF),
        ],
        compiler_params=pltpu.CompilerParams(
            dimension_semantics=("arbitrary",), vmem_limit_bytes=63 * 1024 * 1024
        ),
        name="layer",
    )(live, gathered, images, cotangent)


def shards(params, images, cotangent, live):
    n = lax.axis_size("dp")
    shard = params.shape[0]
    window = up_to((shard + 2 * LANES - 2) // LANES, 16)
    me = lax.axis_index("dp")
    shift = (shard % LANES) * me % LANES
    padded = jnp.pad(params, (0, window * LANES - shard))
    moved = jnp.roll(padded, shift).astype(BF).reshape(window, LANES)
    gathered = lax.all_gather(moved, "dp", axis=0)
    out, din, grads = run_layer(n, shard, window, live, gathered, images, cotangent)
    mine = lax.psum_scatter(
        grads.reshape(n * window, LANES), "dp", scatter_dimension=0, tiled=True
    )
    flat = lax.dynamic_slice(mine.astype(F32).reshape(-1), (shift,), (shard,))
    return out, din, flat


def solution(mesh):
    return jax.shard_map(
        shards,
        mesh=mesh,
        in_specs=(P("dp"), P("dp", None, None), P("dp", None, None), P("dp")),
        out_specs=(P("dp", None, None), P("dp", None, None), P("dp")),
        check_vma=False,
    )
```

profile of v0, /device:TPU:0, one launch (start us, length us, event | category | flops | bytes accessed | tf_op | source)
XLA Modules:
  0.0 295.9 jit_solution(10218935379070815090)
XLA Ops:
  7.2 0.0 all-gather.2.cloned.1.call-start
  7.2 1.0 pad.4
  8.2 1.2 fusion.2
  9.4 0.0 all-gather.2.cloned.1.call-update
  9.4 0.0 copy-start.2
  9.4 0.0 reduce-scatter.2.cloned.1.call-start
  10.2 2.5 copy.11.img_ref
  12.7 0.0 copy-done.2
  12.7 1.2 copy.12.cot_ref
  13.8 60.7 %all-gather.2.cloned.1.call-done.gath_ref = bf16[32,448,128]{2,1,0:T(8,128)(2,1)} async-done(((bf16[1,448,128]{2,1,0:T(8,128)(2,1)}), bf16[32,448,128]{2,1,0:T(8,128)(2,1)}) %all-gather.2.cloned.1.call-update) | async-done | bytes 3670032 | tf_op jit(solution)/shard_map/all_gather | solution.py:296
  74.6 72.4 %layer.1 = (bf16[8,197,384]{2,1,0:T(8,128)(2,1)}, bf16[8,197,384]{2,1,0:T(8,128)(2,1)}, bf16[32,448,128]{2,1,0:T(8,128)(2,1)}) custom-call(s32[1]{0:T(128)S(6)} %copy.15.live_ref, bf16[32,448,128]{2,1,0:T(8,128)(2,1)} %all-gather.2.cloned.1.call-done.gath_ref, bf16[8,197,384]{2,1,0:T(8,128)(2,1)} %copy.11.img_ref, bf16[8,197,384]{2,1,0:T(8,128)(2,1)} %copy.12.cot_ref), custom_call_target="tpu_custom_call" | custom-call | tf_op jit(solution)/shard_map/layer/pallas_call | solution.py:261
  147.0 0.0 copy-start.1
  147.0 0.0 reduce-scatter.2.cloned.1.call-update
  147.1 0.0 copy-start
  147.1 1.2 copy-done.1
  148.3 1.2 copy.13
  149.5 0.0 copy-done
  149.5 1.2 copy.14
  150.7 136.7 %reduce-scatter.2.cloned.1.call-done = bf16[448,128]{1,0:T(8,128)(2,1)} async-done(((bf16[14336,128]{1,0:T(8,128)(2,1)}), bf16[448,128]{1,0:T(8,128)(2,1)}) %reduce-scatter.2.cloned.1.call-update) | async-done | bytes 114704 | tf_op jit(solution)/shard_map/reduce_scatter | solution.py:298
  287.3 1.7 dynamic-slice_convert_fusion
Async XLA Ops:
  7.2 67.4 %all-gather.2.cloned.1.call-start = ((), (), s32[]{:S(2)}) async-start(), calls=%async_computation.1 | async-start | bytes 3784704 | tf_op jit(solution)/shard_map/all_gather | solution.py:296
  9.4 3.3 %copy-start.2 = (bf16[8,197,384]{2,0,1:T(8,128)(2,1)S(1)}, bf16[8,197,384]{2,0,1:T(8,128)(2,1)}, u32[]{:S(2)}) copy-start(bf16[8,197,384]{2,0,1:T(8,128)(2,1)} %param.6) | copy-start | bytes 3631108
  9.4 277.9 %reduce-scatter.2.cloned.1.call-start = ((), (), s32[]{:S(2)}) async-start(), calls=%async_computation.2 | async-start | bytes 3784704 | tf_op jit(solution)/shard_map/reduce_scatter | solution.py:298
  147.0 1.3 copy-start.1
  147.1 2.4 copy-start
Sparse Core Ops, SparseCore 0:
  11.4 63.1 all-gather.1
  147.2 140.1 reduce-scatter.1
where the time goes:
time: 296 us
  waiting for transfers between devices  197 us (67%)
  Pallas kernels  72.4 us (24%)
  between operations  14.8 us (5%)
  local copies, waits for them, and re-layouts  8.22 us (3%)
    reduce_scatter x1, waiting for transfers between devices, shards(): lax.psum_scatter(grads.reshape(n * window, LANES), 'dp', scatter_dimensio...  137 us
    pallas_call x1, Pallas kernels, run_layer(): pl.pallas_call(functools.partial(layer_kernel, n, shard, tok, tokp), grid...  72.4 us
    all_gather x1, waiting for transfers between devices, shards(): gathered = lax.all_gather(moved, 'dp', axis=0)  60.7 us
    unnamed x10, local copies, waits for them, and re-layouts  7.26 us
  transfers between devices with their start and end apart: 2, of which 2 were waited for; matrix products, arithmetic and copies ran while one was open for 2% of the time, Pallas kernels for 0%

commit v1 on v0

--- a/solution.py
+++ b/solution.py
@@ -285,20 +285,205 @@
     )(live, gathered, images, cotangent)
 
 
+PARTS = 4
+MESH = pl.DeviceIdType.MESH
+
+
+def flip(index, mask, bits):
+    for b in range(bits):
+        if mask >> b & 1:
+            index = index + (1 - 2 * (index // (1 << b) % 2)) * (1 << b)
+    return index
+
+
+def part_orders(bits):
+    near = list(range(bits))
+    swapped = near[:1] + near[2:3] + near[1:2] + near[3:]
+    return [near if p % 2 == 0 else swapped for p in range(PARTS)]
+
+
+def mask_of(k, rest):
+    return sum(1 << b for i, b in enumerate(rest) if k >> (len(rest) - 1 - i) & 1)
+
+
+def greet(me, bits):
+    barrier = pltpu.get_barrier_semaphore()
+    for b in range(bits):
+        pl.semaphore_signal(
+            barrier, inc=1, device_id=(flip(me, 1 << b, bits),), device_id_type=MESH
+        )
+    pl.semaphore_wait(barrier, bits)
+
+
+def gather_kernel(bits, x_ref, out_ref, send_sem, recv_sem):
+    me = lax.axis_index("dp")
+    window = x_ref.shape[0]
+    part = window // PARTS
+    orders = [order[::-1] for order in part_orders(bits)]
+    greet(me, bits)
+    sends = []
+
+    def copy(p, source, slot, to, first):
+        rows = pl.ds(p * part, part)
+        return pltpu.make_async_remote_copy(
+            src_ref=x_ref.at[rows] if first else out_ref.at[source, rows],
+            dst_ref=out_ref.at[source, rows],
+            send_sem=send_sem.at[p, slot],
+            recv_sem=recv_sem.at[p, slot],
+            device_id=(to,),
+            device_id_type=MESH,
+        )
+
+    def start(p, s):
+        order = orders[p]
+        to = flip(me, 1 << order[s], bits)
+        for k in range(1 << s):
+            source = flip(me, mask_of(k, order[:s]), bits)
+            c = copy(p, source, (1 << s) - 1 + k, to, k == 0)
+            c.start()
+            sends.append(c)
+
+    def arrive(p, s):
+        order = orders[p]
+        to = flip(me, 1 << order[s], bits)
+        for k in range(1 << s):
+            source = flip(me, mask_of(k, order[:s]) | 1 << order[s], bits)
+            copy(p, source, (1 << s) - 1 + k, to, False).wait_recv()
+
+    for p in range(PARTS):
+        start(p, 0)
+    out_ref[me] = x_ref[...]
+    for s in range(bits):
+        for p in range(PARTS):
+            arrive(p, s)
+            if s + 1 < bits:
+                start(p, s + 1)
+    for c in sends:
+        c.wait_send()
+
+
+def gather(x, n):
+    bits = n.bit_length() - 1
+    return pl.pallas_call(
+        functools.partial(gather_kernel, bits),
+        out_shape=jax.ShapeDtypeStruct((n,) + x.shape, x.dtype),
+        in_specs=[pl.BlockSpec(memory_space=pltpu.VMEM)],
+        out_specs=pl.BlockSpec(memory_space=pltpu.VMEM),
+        scratch_shapes=[
+            pltpu.SemaphoreType.DMA((PARTS, n - 1)),
+            pltpu.SemaphoreType.DMA((PARTS, n - 1)),
+        ],
+        compiler_params=pltpu.CompilerParams(
+            collective_id=1, has_side_effects=True, vmem_limit_bytes=32 * 1024 * 1024
+        ),
+        name="gather",
+    )(x)
+
+
+def reduce_kernel(bits, g_ref, out_ref, acc, recv, send_sem, recv_sem, first_send, first_recv):
+    me = lax.axis_index("dp")
+    half = 1 << (bits - 1)
+    part = g_ref.shape[1] // PARTS
+    orders = part_orders(bits)
+    greet(me, bits)
+    sends = []
+
+    def first_copy(p, k):
+        order = orders[p]
+        block = flip(me, mask_of(k, order[1:]) | 1 << order[0], bits)
+        return pltpu.make_async_remote_copy(
+            src_ref=g_ref.at[block, pl.ds(p * part, part)],
+            dst_ref=recv.at[p, k],
+            send_sem=first_send.at[p, k],
+            recv_sem=first_recv.at[p, k],
+            device_id=(flip(me, 1 << order[0], bits),),
+            device_id_type=MESH,
+        )
+
+    def later_copy(p, s):
+        count = half >> s
+        base = 2 * half - 2 * count
+        return pltpu.make_async_remote_copy(
+            src_ref=acc.at[p, pl.ds(count, count)],
+            dst_ref=recv.at[p, pl.ds(base, count)],
+            send_sem=send_sem.at[p, s],
+            recv_sem=recv_sem.at[p, s],
+            device_id=(flip(me, 1 << orders[p][s], bits),),
+            device_id_type=MESH,
+        )
+
+    for p in range(PARTS):
+        for k in reversed(range(half)):
+            c = first_copy(p, k)
+            c.start()
+            sends.append(c)
+    for s in range(bits):
+        count = half >> s
+        base = 2 * half - 2 * count
+        for p in range(PARTS):
+            rows = pl.ds(p * part, part)
+            if s == 0:
+                for k in reversed(range(half)):
+                    first_copy(p, k).wait_recv()
+                    own = flip(me, mask_of(k, orders[p][1:]), bits)
+                    total = g_ref[own, rows].astype(F32) + recv[p, k].astype(F32)
+                    acc[p, k] = total.astype(BF)
+                    if k == half // 2:
+                        c = later_copy(p, 1)
+                        c.start()
+                        sends.append(c)
+                continue
+            later_copy(p, s).wait_recv()
+            for k in reversed(range(count)):
+                total = acc[p, k].astype(F32) + recv[p, base + k].astype(F32)
+                if s + 1 == bits:
+                    out_ref[rows, :] = total
+                else:
+                    acc[p, k] = total.astype(BF)
+                    if k == count // 2:
+                        c = later_copy(p, s + 1)
+                        c.start()
+                        sends.append(c)
+    for c in sends:
+        c.wait_send()
+
+
+def reduce_windows(grads, n):
+    bits = n.bit_length() - 1
+    window = grads.shape[1]
+    return pl.pallas_call(
+        functools.partial(reduce_kernel, bits),
+        out_shape=jax.ShapeDtypeStruct((window, LANES), F32),
+        in_specs=[pl.BlockSpec(memory_space=pltpu.VMEM)],
+        out_specs=pl.BlockSpec(memory_space=pltpu.VMEM),
+        scratch_shapes=[
+            pltpu.VMEM((PARTS, n // 2, window // PARTS, LANES), BF),
+            pltpu.VMEM((PARTS, n, window // PARTS, LANES), BF),
+            pltpu.SemaphoreType.DMA((PARTS, bits)),
+            pltpu.SemaphoreType.DMA((PARTS, bits)),
+            pltpu.SemaphoreType.DMA((PARTS, n // 2)),
+            pltpu.SemaphoreType.DMA((PARTS, n // 2)),
+        ],
+        compiler_params=pltpu.CompilerParams(
+            collective_id=2, has_side_effects=True, vmem_limit_bytes=40 * 1024 * 1024
+        ),
+        name="reduce",
+    )(grads)
+
+
 def shards(params, images, cotangent, live):
     n = lax.axis_size("dp")
+    assert n & (n - 1) == 0 and n >= 4
     shard = params.shape[0]
-    window = up_to((shard + 2 * LANES - 2) // LANES, 16)
+    window = up_to((shard + 2 * LANES - 2) // LANES, 16 * PARTS)
     me = lax.axis_index("dp")
     shift = (shard % LANES) * me % LANES
     padded = jnp.pad(params, (0, window * LANES - shard))
     moved = jnp.roll(padded, shift).astype(BF).reshape(window, LANES)
-    gathered = lax.all_gather(moved, "dp", axis=0)
+    gathered = gather(moved, n)
     out, din, grads = run_layer(n, shard, window, live, gathered, images, cotangent)
-    mine = lax.psum_scatter(
-        grads.reshape(n * window, LANES), "dp", scatter_dimension=0, tiled=True
-    )
-    flat = lax.dynamic_slice(mine.astype(F32).reshape(-1), (shift,), (shard,))
+    mine = reduce_windows(grads, n)
+    flat = lax.dynamic_slice(mine.reshape(-1), (shift,), (shard,))
     return out, din, flat
 
 

time: 296 us -> 154 us (0.52)
  waiting for transfers between devices: 197 us -> 0 us
  Pallas kernels: 72.4 us -> 138 us
  between operations: 14.8 us -> 1.35 us
  local copies, waits for them, and re-layouts: 8.22 us -> 13.2 us
    reduce_scatter x1 -> x0, waiting for transfers between devices: 137 us -> none  [shards(): lax.psum_scatter(grads.reshape(n * window, LANES), 'dp', scatter_dimensio...]
    pallas_call x0 -> x2, Pallas kernels: none -> 66 us  [the longest x1 34.2 us: gather(): pl.pallas_call(functools.partial(gather_kernel, bits), out_shape=jax.Shap...]
    all_gather x1 -> x0, waiting for transfers between devices: 60.7 us -> none  [shards(): gathered = lax.all_gather(moved, 'dp', axis=0)]
    unnamed x10 -> x12, local copies, waits for them, and re-layouts: 7.26 us -> 11.4 us
  transfers between devices with their start and end apart: 2 -> 0, of which waited for: 2 -> 0; matrix products, arithmetic and copies ran while one was open for 2% -> 0% of each run, Pallas kernels for 0% -> 0%
where the time goes in v1:
time: 154 us
  Pallas kernels  138 us (90%)
  local copies, waits for them, and re-layouts  13.2 us (9%)
    pallas_call x1, Pallas kernels, run_layer(): pl.pallas_call(functools.partial(layer_kernel, n, shard, tok, tokp), grid...  72.5 us
    pallas_call x1, Pallas kernels, gather(): pl.pallas_call(functools.partial(gather_kernel, bits), out_shape=jax.Shap...  34.2 us
    pallas_call x1, Pallas kernels, reduce_windows(): pl.pallas_call(functools.partial(reduce_kernel, bits), out_shape=jax.Shap...  31.7 us
    unnamed x12, local copies, waits for them, and re-layouts  11.4 us

profile of v1, /device:TPU:0, one launch (start us, length us, event | category | flops | bytes accessed | tf_op | source)
XLA Modules:
  0.0 153.5 jit_solution(17563741632893920020)
XLA Ops:
  1.3 1.0 pad.4
  2.3 0.5 fusion.2.x_ref
  2.8 0.0 copy-start.3
  2.8 2.6 %copy.7.img_ref = bf16[8,197,384]{2,1,0:T(8,128)(2,1)} copy(bf16[8,197,384]{2,0,1:T(8,128)(2,1)} %param.5) | data formatting | bytes 2420736 | tf_op args[1]
  5.4 0.0 copy-done.3
  5.4 1.3 copy.8.cot_ref
  6.7 34.2 %gather.1.gath_ref = bf16[32,448,128]{2,1,0:T(8,128)(2,1)S(1)} custom-call(bf16[448,128]{1,0:T(8,128)(2,1)S(1)} %fusion.2.x_ref), custom_call_target="tpu_custom_call" | custom-call | tf_op jit(solution)/shard_map/gather/pallas_call | solution.py:367
  40.9 0.0 copy-start
  40.9 1.8 %copy-done = bf16[32,448,128]{2,1,0:T(8,128)(2,1)} copy-done((bf16[32,448,128]{2,1,0:T(8,128)(2,1)}, bf16[32,448,128]{2,1,0:T(8,128)(2,1)S(1)}, u32[]{:S(2)}) %copy-start) | copy-done | bytes 3670040
  42.7 72.5 %layer.1 = (bf16[8,197,384]{2,1,0:T(8,128)(2,1)}, bf16[8,197,384]{2,1,0:T(8,128)(2,1)}, bf16[32,448,128]{2,1,0:T(8,128)(2,1)}) custom-call(s32[1]{0:T(128)S(6)} %copy.11.live_ref, bf16[32,448,128]{2,1,0:T(8,128)(2,1)} %copy-done, bf16[8,197,384]{2,1,0:T(8,128)(2,1)} %copy.7.img_ref, bf16[8,197,384]{2,1,0:T(8,128)(2,1)} %copy.8.cot_ref), custom_call_target="tpu_custom_call" | custom-call | tf_op jit(solution)/shard_map/layer/pallas_call | solution.py:261
  115.2 2.5 %copy.9 = bf16[8,197,384]{2,0,1:T(8,128)(2,1)} copy(bf16[8,197,384]{2,1,0:T(8,128)(2,1)} %get-tuple-element.9) | data formatting | bytes 2420736
  117.7 0.0 copy-start.1
  117.7 2.0 %copy-done.1 = bf16[32,448,128]{2,1,0:T(8,128)(2,1)S(1)} copy-done((bf16[32,448,128]{2,1,0:T(8,128)(2,1)S(1)}, bf16[32,448,128]{2,1,0:T(8,128)(2,1)}, u32[]{:S(2)}) %copy-start.1) | copy-done | bytes 3670040
  119.7 0.0 copy-start.2
  119.7 31.7 %reduce.1 = f32[448,128]{1,0:T(8,128)S(1)} custom-call(bf16[32,448,128]{2,1,0:T(8,128)(2,1)S(1)} %copy-done.1), custom_call_target="tpu_custom_call" | custom-call | tf_op jit(solution)/shard_map/reduce/pallas_call | solution.py:454
  151.5 0.8 dynamic_slice.8
  152.3 0.0 copy-done.2
  152.3 1.2 copy.10
Async XLA Ops:
  2.8 2.6 %copy-start.3 = (bf16[8,197,384]{2,0,1:T(8,128)(2,1)S(1)}, bf16[8,197,384]{2,0,1:T(8,128)(2,1)}, u32[]{:S(2)}) copy-start(bf16[8,197,384]{2,0,1:T(8,128)(2,1)} %param.6) | copy-start | bytes 3631108
  40.9 1.8 %copy-start = (bf16[32,448,128]{2,1,0:T(8,128)(2,1)}, bf16[32,448,128]{2,1,0:T(8,128)(2,1)S(1)}, u32[]{:S(2)}) copy-start(bf16[32,448,128]{2,1,0:T(8,128)(2,1)S(1)} %gather.1.gath_ref) | copy-start | bytes 11010052
  117.7 2.0 %copy-start.1 = (bf16[32,448,128]{2,1,0:T(8,128)(2,1)S(1)}, bf16[32,448,128]{2,1,0:T(8,128)(2,1)}, u32[]{:S(2)}) copy-start(bf16[32,448,128]{2,1,0:T(8,128)(2,1)} %get-tuple-element.8.g_ref) | copy-start | bytes 11010052
  119.7 32.6 %copy-start.2 = (bf16[8,197,384]{2,1,0:T(8,128)(2,1)S(1)}, bf16[8,197,384]{2,1,0:T(8,128)(2,1)}, u32[]{:S(2)}) copy-start(bf16[8,197,384]{2,1,0:T(8,128)(2,1)} %get-tuple-element.10) | copy-start | bytes 3631108

commit v2 on v1

--- a/solution.py
+++ b/solution.py
@@ -27,7 +27,7 @@
 VEC_ROWS = (0, 1, ROW_OUT - 2, ROW_OUT - 1, ROW_UP - 3, ROW_UP - 2, ROW_UP - 1, ROW_BDOWN)
 G1, S1, BQ, BV, BO, G2, S2, BD = range(8)
 
-GROUP = 2
+GROUP = 4
 CHUNK = 512
 
 
@@ -299,7 +299,10 @@
 def part_orders(bits):
     near = list(range(bits))
     swapped = near[:1] + near[2:3] + near[1:2] + near[3:]
-    return [near if p % 2 == 0 else swapped for p in range(PARTS)]
+    orders = [near, swapped]
+    for order in (near, swapped):
+        orders.append(order[:2] + order[3:4] + order[2:3] + order[4:])
+    return orders
 
 
 def mask_of(k, rest):

time: 154 us -> 148 us (0.961)
  Pallas kernels: 138 us -> 132 us
    pallas_call x1, Pallas kernels: 72.5 us -> 69.8 us  [run_layer(): pl.pallas_call(functools.partial(layer_kernel, n, shard, tok, tokp), grid...]
    pallas_call x1, Pallas kernels: 34.2 us -> 32 us  [gather(): pl.pallas_call(functools.partial(gather_kernel, bits), out_shape=jax.Shap...]
where the time goes in v2:
time: 148 us; the launch traced here: 147 us
  Pallas kernels  132 us (89%)
  local copies, waits for them, and re-layouts  13.1 us (9%)
    pallas_call x1, Pallas kernels, run_layer(): pl.pallas_call(functools.partial(layer_kernel, n, shard, tok, tokp), grid...  69.8 us
    pallas_call x1, Pallas kernels, gather(): pl.pallas_call(functools.partial(gather_kernel, bits), out_shape=jax.Shap...  32 us
    pallas_call x1, Pallas kernels, reduce_windows(): pl.pallas_call(functools.partial(reduce_kernel, bits), out_shape=jax.Shap...  30.5 us
    unnamed x12, local copies, waits for them, and re-layouts  11.4 us

profile of v2, /device:TPU:0, one launch (start us, length us, event | category | flops | bytes accessed | tf_op | source)
XLA Modules:
  0.0 147.3 jit_solution(6927577442880554095)
XLA Ops:
  1.3 1.0 pad.4
  2.3 0.5 fusion.2.x_ref
  2.8 0.0 copy-start.3
  2.8 2.6 %copy.7.img_ref = bf16[8,197,384]{2,1,0:T(8,128)(2,1)} copy(bf16[8,197,384]{2,0,1:T(8,128)(2,1)} %param.5) | data formatting | bytes 2420736 | tf_op args[1]
  5.4 0.0 copy-done.3
  5.4 1.3 copy.8.cot_ref
  6.7 32.0 %gather.1.gath_ref = bf16[32,448,128]{2,1,0:T(8,128)(2,1)S(1)} custom-call(bf16[448,128]{1,0:T(8,128)(2,1)S(1)} %fusion.2.x_ref), custom_call_target="tpu_custom_call" | custom-call | tf_op jit(solution)/shard_map/gather/pallas_call | solution.py:370
  38.7 0.0 copy-start
  38.7 1.8 %copy-done = bf16[32,448,128]{2,1,0:T(8,128)(2,1)} copy-done((bf16[32,448,128]{2,1,0:T(8,128)(2,1)}, bf16[32,448,128]{2,1,0:T(8,128)(2,1)S(1)}, u32[]{:S(2)}) %copy-start) | copy-done | bytes 3670040
  40.5 69.8 %layer.1 = (bf16[8,197,384]{2,1,0:T(8,128)(2,1)}, bf16[8,197,384]{2,1,0:T(8,128)(2,1)}, bf16[32,448,128]{2,1,0:T(8,128)(2,1)}) custom-call(s32[1]{0:T(128)S(6)} %copy.11.live_ref, bf16[32,448,128]{2,1,0:T(8,128)(2,1)} %copy-done, bf16[8,197,384]{2,1,0:T(8,128)(2,1)} %copy.7.img_ref, bf16[8,197,384]{2,1,0:T(8,128)(2,1)} %copy.8.cot_ref), custom_call_target="tpu_custom_call" | custom-call | tf_op jit(solution)/shard_map/layer/pallas_call | solution.py:261
  110.3 2.5 %copy.9 = bf16[8,197,384]{2,0,1:T(8,128)(2,1)} copy(bf16[8,197,384]{2,1,0:T(8,128)(2,1)} %get-tuple-element.9) | data formatting | bytes 2420736
  112.8 0.0 copy-start.1
  112.8 2.0 %copy-done.1 = bf16[32,448,128]{2,1,0:T(8,128)(2,1)S(1)} copy-done((bf16[32,448,128]{2,1,0:T(8,128)(2,1)S(1)}, bf16[32,448,128]{2,1,0:T(8,128)(2,1)}, u32[]{:S(2)}) %copy-start.1) | copy-done | bytes 3670040
  114.8 0.0 copy-start.2
  114.8 30.5 %reduce.1 = f32[448,128]{1,0:T(8,128)S(1)} custom-call(bf16[32,448,128]{2,1,0:T(8,128)(2,1)S(1)} %copy-done.1), custom_call_target="tpu_custom_call" | custom-call | tf_op jit(solution)/shard_map/reduce/pallas_call | solution.py:457
  145.3 0.8 dynamic_slice.8
  146.1 0.0 copy-done.2
  146.1 1.2 copy.10
Async XLA Ops:
  2.8 2.6 %copy-start.3 = (bf16[8,197,384]{2,0,1:T(8,128)(2,1)S(1)}, bf16[8,197,384]{2,0,1:T(8,128)(2,1)}, u32[]{:S(2)}) copy-start(bf16[8,197,384]{2,0,1:T(8,128)(2,1)} %param.6) | copy-start | bytes 3631108
  38.7 1.8 %copy-start = (bf16[32,448,128]{2,1,0:T(8,128)(2,1)}, bf16[32,448,128]{2,1,0:T(8,128)(2,1)S(1)}, u32[]{:S(2)}) copy-start(bf16[32,448,128]{2,1,0:T(8,128)(2,1)S(1)} %gather.1.gath_ref) | copy-start | bytes 11010052
  112.8 2.0 %copy-start.1 = (bf16[32,448,128]{2,1,0:T(8,128)(2,1)S(1)}, bf16[32,448,128]{2,1,0:T(8,128)(2,1)}, u32[]{:S(2)}) copy-start(bf16[32,448,128]{2,1,0:T(8,128)(2,1)} %get-tuple-element.8.g_ref) | copy-start | bytes 11010052
  114.8 31.3 %copy-start.2 = (bf16[8,197,384]{2,1,0:T(8,128)(2,1)S(1)}, bf16[8,197,384]{2,1,0:T(8,128)(2,1)}, u32[]{:S(2)}) copy-start(bf16[8,197,384]{2,1,0:T(8,128)(2,1)} %get-tuple-element.10) | copy-start | bytes 3631108
